TPU v7x, 32 devices: a whole 2x2x4 slice. The times are simulated.
32 devices in a mesh: leaf: 8 (over z, y), front: 4 (over x, core).
Axes of the slice: x: 2, y: 2, z: 4, core: 2. Of those that a mesh axis runs over, the one named last changes fastest.
Arguments:
- rhs_local: float32 [256, 256, 256], P(('leaf', 'front')), may hold values from -6 to 6
- dinv_local: float32 [256, 256, 256], P(('leaf', 'front')), may hold values from -1 to 2
- update_local: float32 [256, 256, 256], P(('leaf', 'front')), may hold values from -0.25 to 0.25
- parent: int32 [256], P(('leaf', 'front')), may hold values from 1 to 8, as said below
- row_blocks: int32 [256, 256], P(('leaf', 'front')), may hold values from 0 to 255, each once within a row
- sep_rhs: float32 [2048, 256], P(('leaf', 'front')), may hold values from -6 to 6
- sep_dinv: float32 [2048, 256], P(('leaf', 'front')), may hold values from -1 to 2
- sep_coupling: float32 [2048, 256], P(('leaf', 'front')), may hold values from -2 to 1
Outputs:
- sol_local: float32 [256, 256, 256], P(('leaf', 'front'))
- sep_solution: float32 [2048, 256], P(('leaf', 'front'))
Inputs may be any that keep to these rules, and one draw needn't show every extreme that they name: parent_k is the position of supernode k's parent within the same block of 8, always greater than k; the value 8 names the block's separator. `row_blocks`: each row is a permutation of 0 .. 255.
All inputs are finite; a program needn't handle non-finite values.
Results may differ from a plain program's by a relative error of at most 0.00024.
Values sent between devices are 32-bit elements; how exact they have to be, the bound alone decides.
No kernel may reach another device: no remote copies, remote signals or barrier semaphores. Data moves between devices by JAX's collectives and lax.ppermute only.
A program may use at most 128 MiB of HBM per device.

v0:
```python
import jax
import jax.numpy as jnp
from jax import lax
from jax.sharding import PartitionSpec as P


def entering(part, axis, combine, identity, reverse):
    count = lax.axis_size(axis)
    place = lax.axis_index(axis)
    ahead = count - 1 - place if reverse else place
    gathered = jax.tree.map(lambda a: lax.all_gather(a, axis), part)
    state = jax.tree.map(lambda a, e: jnp.zeros_like(a) + jnp.asarray(e, a.dtype), part, identity)

    def one(lap, state):
        source = count - 1 - lap if reverse else lap
        return combine(
            state, jax.tree.map(lambda a: lax.dynamic_index_in_dim(a, source, 0, False), gathered)
        )

    return lax.fori_loop(0, ahead, one, state)


def matmul(left, right):
    return jnp.dot(left, right, preferred_element_type=jnp.float32, precision=lax.Precision.HIGHEST)


def matmul_t(left, right):
    return lax.dot_general(
        left,
        right,
        (((0,), (0,)), ((), ())),
        precision=lax.Precision.HIGHEST,
        preferred_element_type=jnp.float32,
    )


def compose_ahead(earlier, latter):
    return (matmul(latter[0], earlier[0]), matmul(latter[0], earlier[1]) + latter[1])


def compose_back(earlier, latter):
    return (matmul(earlier[0], latter[0]), matmul_t(latter[0], earlier[1]) + latter[1])


def forward_block(rhs_block, inverse, update, parent_block, row_index):
    count_nodes = rhs_block.shape[0]
    pending = jnp.zeros((count_nodes + 1,) + rhs_block.shape[1:], jnp.float32)
    finished_solution = jnp.zeros(rhs_block.shape, jnp.float32)

    def advance(step_no, state_pair):
        pending_rows, finished_rows = state_pair
        solved_node = matmul(inverse[step_no], rhs_block[step_no] - pending_rows[step_no])
        update_rows = jnp.take(matmul(update[step_no], solved_node), row_index[step_no], axis=0)
        pending_rows = pending_rows.at[parent_block[step_no]].add(update_rows)
        return (pending_rows, finished_rows.at[step_no].set(solved_node))

    pending, finished_solution = lax.fori_loop(
        0, count_nodes, advance, (pending, finished_solution)
    )
    return (finished_solution, pending[count_nodes])


def backward_block(finished_solution, inverse, update, parent_block, row_index, top_value):
    count_nodes = finished_solution.shape[0]
    known_rows = jnp.concatenate(
        [jnp.zeros(finished_solution.shape, jnp.float32), top_value[None]], axis=0
    )

    def retreat(step_no, known_state):
        node_pos = count_nodes - 1 - step_no
        parent_value = known_state[parent_block[node_pos]]
        placed = (
            jnp.zeros(parent_value.shape, jnp.float32).at[row_index[node_pos]].set(parent_value)
        )
        result = matmul_t(
            inverse[node_pos], finished_solution[node_pos] - matmul_t(update[node_pos], placed)
        )
        return known_state.at[node_pos].set(result)

    known_rows = lax.fori_loop(0, count_nodes, retreat, known_rows)
    return known_rows[:count_nodes]


def local(rhs_local, dinv_local, update_local, parent, row_blocks, sep_rhs, sep_dinv, sep_coupling):
    finished_solution, top_term = forward_block(
        rhs_local, dinv_local, update_local, parent, row_blocks
    )
    front_pos = lax.axis_index("front")
    share_rows = sep_rhs.shape[0]
    block_order = sep_dinv.shape[1]
    drive_share = sep_rhs - lax.psum_scatter(top_term, "front", scatter_dimension=0, tiled=True)
    coupling, drive_full = (
        lax.all_gather(sep_coupling, "front", axis=0, tiled=True),
        lax.all_gather(drive_share, "front", axis=0, tiled=True),
    )
    chain_map, drive_term = (
        lax.all_gather(-matmul(sep_dinv, coupling), "front", axis=0, tiled=True),
        lax.all_gather(matmul(sep_dinv, drive_full), "front", axis=0, tiled=True),
    )
    unit_map = jnp.eye(block_order, dtype=jnp.float32)
    previous = entering(
        (chain_map, drive_term),
        "leaf",
        compose_ahead,
        (unit_map, jnp.zeros_like(drive_term)),
        False,
    )[1]
    forward_top = matmul(chain_map, previous) + drive_term
    back_drive = -matmul_t(chain_map, forward_top)
    following = entering(
        (chain_map, back_drive), "leaf", compose_back, (unit_map, jnp.zeros_like(back_drive)), True
    )[1]
    residue = forward_top - following
    own_residue = lax.dynamic_slice_in_dim(residue, front_pos * share_rows, share_rows, 0)
    top_value = lax.psum(matmul_t(sep_dinv, own_residue), "front")
    sep_solution = lax.dynamic_slice_in_dim(top_value, front_pos * share_rows, share_rows, 0)
    sol_local = backward_block(
        finished_solution, dinv_local, update_local, parent, row_blocks, top_value
    )
    return (sol_local, sep_solution)


def solution(mesh):
    placed = (
        P(("leaf", "front"), None, None),
        P(("leaf", "front"), None, None),
        P(("leaf", "front"), None, None),
        P(("leaf", "front")),
        P(("leaf", "front"), None),
        P(("leaf", "front"), None),
        P(("leaf", "front"), None),
        P(("leaf", "front"), None),
    )
    return jax.shard_map(
        local,
        mesh=mesh,
        in_specs=placed,
        out_specs=(P(("leaf", "front"), None, None), P(("leaf", "front"), None)),
        check_vma=False,
    )
```

profile of v0, /device:TPU:0, one launch (start us, length us, event | category | flops | bytes accessed | tf_op | source)
XLA Modules:
  0.0 391.7 jit_solution(16533572137065074752)
XLA Ops:
  9.8 79.2 %while.59 = (s32[]{:T(128)}, f32[9,256,256]{2,1,0:T(8,128)S(1)}, f32[8,256,256]{2,1,0:T(8,128)}, s32[8]{0:T(128)S(1)}, s32[8,256]{1,0:T(8,128)}, /*index=5*/f32[...) while((s32[]{:T(128)}, f32[9,256,256]{2,1,0:T(8,128)S(1)}, ...), condition=%wide.region_3.4_spmd, body=%wide.region_0.3_spmd.sunk | while | flops 402984224 | bytes 3683810 | solution.py:57
  13.1 2.8 fusion.67
  23.0 2.8 fusion.67
  32.9 2.8 fusion.67
  42.8 2.8 fusion.67
  52.7 2.8 fusion.67
  62.6 2.8 fusion.67
  72.5 2.8 fusion.67
  82.4 2.8 fusion.67
  89.9 7.2 %all_gather.32 = f32[256,256]{1,0:T(8,128)S(1)} all-gather(f32[64,256]{1,0:T(8,128)S(1)} %copy-done.3), channel_id=1, replica_groups=mesh['leaf'=8,'front'=4] {'front'}, dimensions={0}, use_global_device_ids=true | all-gather | bytes 327680 | tf_op jit(solution)/shard_map/all_gather | solution.py:93
  97.3 6.3 %all_gather.33 = f32[256,256]{1,0:T(8,128)} all-gather(f32[64,256]{1,0:T(8,128)S(1)} %convolution_negate_fusion.1), channel_id=1, replica_groups=mesh['leaf'=8,'front'=4] {'front'}, dimensions={0}, use_global_device_ids=true | all-gather | bytes 327680 | tf_op jit(solution)/shard_map/all_gather | solution.py:97
  103.7 9.0 %reduce-scatter.2.cloned.1.call-done = f32[64,256]{1,0:T(8,128)} async-done(((f32[256,256]{1,0:T(8,128)}), f32[64,256]{1,0:T(8,128)}) %reduce-scatter.2.cloned.1.call-update) | async-done | bytes 65552 | tf_op jit(solution)/shard_map/reduce_scatter | solution.py:91
  113.5 5.8 %all_gather.36 = f32[256,256]{1,0:T(8,128)S(1)} all-gather(f32[64,256]{1,0:T(8,128)S(1)} %sub.46), channel_id=1, replica_groups=mesh['leaf'=8,'front'=4] {'front'}, dimensions={0}, use_global_device_ids=true | all-gather | bytes 327680 | tf_op jit(solution)/shard_map/all_gather | solution.py:94
  119.6 6.3 %all_gather.37 = f32[256,256]{1,0:T(8,128)} all-gather(f32[64,256]{1,0:T(8,128)S(1)} %convolution_bitcast_fusion.2), channel_id=1, replica_groups=mesh['leaf'=8,'front'=4] {'front'}, dimensions={0}, use_global_device_ids=true | all-gather | bytes 327680 | tf_op jit(solution)/shard_map/all_gather | solution.py:98
  126.0 28.4 %all-gather.7.cloned.1.call-done = f32[2048,256]{1,0:T(8,128)} async-done(((f32[256,256]{1,0:T(8,128)}), f32[2048,256]{1,0:T(8,128)}) %all-gather.7.cloned.1.call-update) | async-done | bytes 2097168 | tf_op jit(solution)/shard_map/all_gather | solution.py:11
  154.4 49.9 %all-gather.9.cloned.1.call-done = f32[2048,256]{1,0:T(8,128)} async-done(((f32[256,256]{1,0:T(8,128)}), f32[2048,256]{1,0:T(8,128)}) %all-gather.9.cloned.1.call-update) | async-done | bytes 2097168 | tf_op jit(solution)/shard_map/all_gather | solution.py:11
  207.2 57.1 %all-gather.11.cloned.1.call-done = f32[2048,256]{1,0:T(8,128)} async-done(((f32[256,256]{1,0:T(8,128)}), f32[2048,256]{1,0:T(8,128)}) %all-gather.11.cloned.1.call-update) | async-done | bytes 2097168 | tf_op jit(solution)/shard_map/all_gather | solution.py:11
  264.3 11.9 %while.61 = (s32[]{:T(128)}, f32[256,256]{1,0:T(8,128)S(1)}, s32[]{:T(128)}, f32[8,256,256]{2,1,0:T(8,128)}, f32[8,256,256]{2,1,0:T(8,128)}, /*index=5*/s32[]{:T(128)}, s32[]{:T(128)}, s32[]{:T(128)}, s32[]{:T(128)}) while((s32[]{:T(128)}, f32[256,256]{1,0:T(8,128)S(1)}, s32[]{:T(128)}, f32[8,256,256]{2,1,0:T(8,128)}, ...), condition=%wide.region_8.9_spmd, body=%wide.region_7.8_spmd.sunk | while | flops 201392128 | bytes 1574027 | solution.py:20
  264.4 1.6 convolution_add_fusion.6
  266.1 1.6 convolution_add_fusion.6
  267.8 1.6 convolution_add_fusion.6
  271.2 1.6 convolution_add_fusion.6
  277.4 29.3 %all-reduce.3.cloned.1.call-done = f32[256,256]{0,1:T(8,128)} async-done(((f32[256,256]{0,1:T(8,128)}), f32[256,256]{0,1:T(8,128)}) %all-reduce.3.cloned.1.call-update) | async-done | bytes 262160 | tf_op jit(solution)/shard_map/psum | solution.py:115
  309.7 72.8 %while.62 = (s32[]{:T(128)}, f32[9,256,256]{2,1,0:T(8,128)S(1)}, f32[8,256,256]{2,1,0:T(8,128)}, f32[8,256,256]{2,1,0:T(8,128)}, f32[8,256,256]{2,1,0:T(8,128)},...) while((s32[]{:T(128)}, f32[9,256,256]{2,1,0:T(8,128)S(1)}, ...), condition=%wide.region_13.14_spmd, body=%wide.region_10.13_spmd.sunk | while | flops 402785056 | bytes 2625843 | solution.py:80
  316.6 2.2 fusion.80
  325.7 2.2 fusion.80
  334.8 2.2 fusion.80
  343.9 2.2 fusion.80
  353.0 2.2 fusion.80
  362.1 2.2 fusion.80
  371.2 2.2 fusion.80
  380.3 2.2 fusion.80
  (157 shorter events, 100.1 us)
Async XLA Ops:
  8.0 89.1 %copy-start = (f32[64,256]{1,0:T(8,128)S(1)}, f32[64,256]{1,0:T(8,128)}, u32[]{:S(2)}) copy-start(f32[64,256]{1,0:T(8,128)} %param.28) | copy-start | bytes 196612
  8.0 104.7 %reduce-scatter.2.cloned.1.call-start = ((), (), s32[]{:S(2)}) async-start(), calls=%async_computation.1 | async-start | bytes 327680 | tf_op jit(solution)/shard_map/reduce_scatter | solution.py:91
  8.1 1.7 copy-start.5
  8.1 1.7 copy-start.6
  8.1 1.7 copy-start.7
  9.8 80.1 %copy-start.3 = (f32[64,256]{1,0:T(8,128)S(1)}, f32[64,256]{1,0:T(8,128)}, u32[]{:S(2)}) copy-start(f32[64,256]{1,0:T(8,128)} %param.29) | copy-start | bytes 196612
  89.1 23.6 %copy-start.4 = (f32[64,256]{1,0:T(8,128)S(1)}, f32[64,256]{1,0:T(8,128)}, u32[]{:S(2)}) copy-start(f32[64,256]{1,0:T(8,128)} %param.27) | copy-start | bytes 196612
  89.8 64.6 %all-gather.7.cloned.1.call-start = ((), (), s32[]{:S(2)}) async-start(), calls=%async_computation.3 | async-start | bytes 2359296 | tf_op jit(solution)/shard_map/all_gather | solution.py:11
  103.7 100.7 %all-gather.9.cloned.1.call-start = ((), (), s32[]{:S(2)}) async-start(), calls=%async_computation.4 | async-start | bytes 2359296 | tf_op jit(solution)/shard_map/all_gather | solution.py:11
  125.9 138.4 %all-gather.11.cloned.1.call-start = ((), (), s32[]{:S(2)}) async-start(), calls=%async_computation.5 | async-start | bytes 2359296 | tf_op jit(solution)/shard_map/all_gather | solution.py:11
  204.4 1.0 copy-start.1
  204.4 1.0 copy-start.2
  207.1 99.6 %all-reduce.3.cloned.1.call-start = ((), (), s32[]{:S(2)}) async-start(), calls=%async_computation.2 | async-start | bytes 524288 | tf_op jit(solution)/shard_map/psum | solution.py:115
Sparse Core Ops, SparseCore 0:
  89.9 22.7 reduce-scatter.1
  277.5 29.1 all-reduce.2
Sparse Core Ops, SparseCore 1:
  103.7 50.6 all-gather.6
  156.6 47.7 all-gather.8
  207.2 57.1 all-gather.10
where the time goes:
time: 394 us; the launch traced here: 392 us
  waiting for transfers between devices  174 us (44%)
  matrix products  78.4 us (20%)
  local copies, waits for them, and re-layouts  37.6 us (10%)
  other arithmetic  30.3 us (8%)
  loops' own time  29.8 us (8%)
  blocking collectives  25.6 us (6%)
  between operations  15.8 us (4%)
    all_gather x3, waiting for transfers between devices, entering(): gathered = jax.tree.map(lambda a: lax.all_gather(a, axis), part)  136 us
    dot_general x25, matrix products, matmul_t(): lax.dot_general(left, right, (((0,), (0,)), ((), ())), precision=lax.Prec...  44.3 us
    dot_general x19, matrix products, matmul(): jnp.dot(left, right, preferred_element_type=jnp.float32, precision=lax.Pr...  34.1 us
    psum x1, waiting for transfers between devices, local(): top_value = lax.psum(matmul_t(sep_dinv, own_residue), 'front')  29.3 us
    another operation x1, loops' own time, forward_block(): lax.fori_loop(0, count_nodes, advance, (pending, finished_solution))  15.5 us
    another operation x1, loops' own time, backward_block(): known_rows = lax.fori_loop(0, count_nodes, retreat, known_rows)  14 us
    another operation x16, other arithmetic  12.1 us
    scatter x8, local copies, waits for them, and re-layouts, retreat(): jnp.zeros(parent_value.shape, jnp.float32).at[row_index[node_pos]]  12 us
  transfers between devices with their start and end apart: 5, of which 5 were waited for; matrix products, arithmetic and copies ran while one was open for 0% of the time, Pallas kernels for 0%

commit v1 on v0

--- a/solution.py
+++ b/solution.py
@@ -112,7 +112,7 @@
     )[1]
     residue = forward_top - following
     own_residue = lax.dynamic_slice_in_dim(residue, front_pos * share_rows, share_rows, 0)
-    top_value = lax.psum(matmul_t(sep_dinv, own_residue), "front")
+    top_value = jnp.sum(lax.all_gather(matmul_t(sep_dinv, own_residue), "front"), axis=0)
     sep_solution = lax.dynamic_slice_in_dim(top_value, front_pos * share_rows, share_rows, 0)
     sol_local = backward_block(
         finished_solution, dinv_local, update_local, parent, row_blocks, top_value

time: 394 us -> 379 us (0.962)
  waiting for transfers between devices: 174 us -> 159 us
    psum x1 -> x0, waiting for transfers between devices: 29.3 us -> none  [local(): top_value = lax.psum(matmul_t(sep_dinv, own_residue), 'front')]
    all_gather x0 -> x1, waiting for transfers between devices: none -> 14.1 us  [local(): lax.all_gather(matmul_t(sep_dinv, own_residue), 'front')]
where the time goes in v1:
time: 379 us; the launch traced here: 377 us
  waiting for transfers between devices  159 us (42%)
  matrix products  78.4 us (21%)
  local copies, waits for them, and re-layouts  37.5 us (10%)
  other arithmetic  30.9 us (8%)
  loops' own time  29.8 us (8%)
  blocking collectives  25.6 us (7%)
  between operations  15.9 us (4%)
    all_gather x3, waiting for transfers between devices, entering(): gathered = jax.tree.map(lambda a: lax.all_gather(a, axis), part)  136 us
    dot_general x25, matrix products, matmul_t(): lax.dot_general(left, right, (((0,), (0,)), ((), ())), precision=lax.Prec...  44.3 us
    dot_general x19, matrix products, matmul(): jnp.dot(left, right, preferred_element_type=jnp.float32, precision=lax.Pr...  34.1 us
    another operation x1, loops' own time, forward_block(): lax.fori_loop(0, count_nodes, advance, (pending, finished_solution))  15.5 us
    all_gather x1, waiting for transfers between devices, local(): lax.all_gather(matmul_t(sep_dinv, own_residue), 'front')  14.1 us
    another operation x1, loops' own time, backward_block(): known_rows = lax.fori_loop(0, count_nodes, retreat, known_rows)  14 us
    another operation x16, other arithmetic  12.1 us
    scatter x8, local copies, waits for them, and re-layouts, retreat(): jnp.zeros(parent_value.shape, jnp.float32).at[row_index[node_pos]]  12 us
  transfers between devices with their start and end apart: 5, of which 5 were waited for; matrix products, arithmetic and copies ran while one was open for 0% of the time, Pallas kernels for 0%

profile of v1, /device:TPU:0, one launch (start us, length us, event | category | flops | bytes accessed | tf_op | source)
XLA Modules:
  0.0 376.9 jit_solution(14664386184688474829)
XLA Ops:
  9.8 79.2 %while.59 = (s32[]{:T(128)}, f32[9,256,256]{2,1,0:T(8,128)S(1)}, f32[8,256,256]{2,1,0:T(8,128)}, s32[8]{0:T(128)S(1)}, s32[8,256]{1,0:T(8,128)}, /*index=5*/f32[...) while((s32[]{:T(128)}, f32[9,256,256]{2,1,0:T(8,128)S(1)}, ...), condition=%wide.region_3.4_spmd, body=%wide.region_0.3_spmd.sunk | while | flops 402984224 | bytes 3683810 | solution.py:57
  13.1 2.8 fusion.67
  23.0 2.8 fusion.67
  32.9 2.8 fusion.67
  42.8 2.8 fusion.67
  52.7 2.8 fusion.67
  62.6 2.8 fusion.67
  72.5 2.8 fusion.67
  82.4 2.8 fusion.67
  89.9 7.2 %all_gather.38 = f32[256,256]{1,0:T(8,128)S(1)} all-gather(f32[64,256]{1,0:T(8,128)S(1)} %copy-done.3), channel_id=1, replica_groups=mesh['leaf'=8,'front'=4] {'front'}, dimensions={0}, use_global_device_ids=true | all-gather | bytes 327680 | tf_op jit(solution)/shard_map/all_gather | solution.py:93
  97.3 6.3 %all_gather.39 = f32[256,256]{1,0:T(8,128)} all-gather(f32[64,256]{1,0:T(8,128)S(1)} %convolution_negate_fusion.1), channel_id=1, replica_groups=mesh['leaf'=8,'front'=4] {'front'}, dimensions={0}, use_global_device_ids=true | all-gather | bytes 327680 | tf_op jit(solution)/shard_map/all_gather | solution.py:97
  103.7 9.0 %reduce-scatter.2.cloned.1.call-done = f32[64,256]{1,0:T(8,128)} async-done(((f32[256,256]{1,0:T(8,128)}), f32[64,256]{1,0:T(8,128)}) %reduce-scatter.2.cloned.1.call-update) | async-done | bytes 65552 | tf_op jit(solution)/shard_map/reduce_scatter | solution.py:91
  113.5 5.8 %all_gather.42 = f32[256,256]{1,0:T(8,128)S(1)} all-gather(f32[64,256]{1,0:T(8,128)S(1)} %sub.46), channel_id=1, replica_groups=mesh['leaf'=8,'front'=4] {'front'}, dimensions={0}, use_global_device_ids=true | all-gather | bytes 327680 | tf_op jit(solution)/shard_map/all_gather | solution.py:94
  119.6 6.3 %all_gather.43 = f32[256,256]{1,0:T(8,128)} all-gather(f32[64,256]{1,0:T(8,128)S(1)} %convolution_bitcast_fusion.2), channel_id=1, replica_groups=mesh['leaf'=8,'front'=4] {'front'}, dimensions={0}, use_global_device_ids=true | all-gather | bytes 327680 | tf_op jit(solution)/shard_map/all_gather | solution.py:98
  126.0 28.4 %all-gather.9.cloned.1.call-done = f32[2048,256]{1,0:T(8,128)} async-done(((f32[256,256]{1,0:T(8,128)}), f32[2048,256]{1,0:T(8,128)}) %all-gather.9.cloned.1.call-update) | async-done | bytes 2097168 | tf_op jit(solution)/shard_map/all_gather | solution.py:11
  154.4 49.9 %all-gather.11.cloned.1.call-done = f32[2048,256]{1,0:T(8,128)} async-done(((f32[256,256]{1,0:T(8,128)}), f32[2048,256]{1,0:T(8,128)}) %all-gather.11.cloned.1.call-update) | async-done | bytes 2097168 | tf_op jit(solution)/shard_map/all_gather | solution.py:11
  207.2 57.1 %all-gather.13.cloned.1.call-done = f32[2048,256]{1,0:T(8,128)} async-done(((f32[256,256]{1,0:T(8,128)}), f32[2048,256]{1,0:T(8,128)}) %all-gather.13.cloned.1.call-update) | async-done | bytes 2097168 | tf_op jit(solution)/shard_map/all_gather | solution.py:11
  264.3 11.9 %while.61 = (s32[]{:T(128)}, f32[256,256]{1,0:T(8,128)S(1)}, s32[]{:T(128)}, f32[8,256,256]{2,1,0:T(8,128)}, f32[8,256,256]{2,1,0:T(8,128)}, /*index=5*/s32[]{:T(128)}, s32[]{:T(128)}, s32[]{:T(128)}, s32[]{:T(128)}) while((s32[]{:T(128)}, f32[256,256]{1,0:T(8,128)S(1)}, s32[]{:T(128)}, f32[8,256,256]{2,1,0:T(8,128)}, ...), condition=%wide.region_8.9_spmd, body=%wide.region_7.8_spmd.sunk | while | flops 201392128 | bytes 1574027 | solution.py:20
  264.4 1.6 convolution_add_fusion.6
  267.8 1.6 convolution_add_fusion.6
  272.9 1.6 convolution_add_fusion.6
  277.4 14.1 %all-gather.15.cloned.1.call-done = f32[1024,256]{0,1:T(8,128)} async-done(((f32[256,256]{0,1:T(8,128)}), f32[1024,256]{0,1:T(8,128)}) %all-gather.15.cloned.1.call-update) | async-done | bytes 1048592 | tf_op jit(solution)/shard_map/all_gather | solution.py:115
  291.5 1.7 reshape.299
  295.0 72.8 %while.62 = (s32[]{:T(128)}, f32[9,256,256]{2,1,0:T(8,128)S(1)}, f32[8,256,256]{2,1,0:T(8,128)}, f32[8,256,256]{2,1,0:T(8,128)}, f32[8,256,256]{2,1,0:T(8,128)},...) while((s32[]{:T(128)}, f32[9,256,256]{2,1,0:T(8,128)S(1)}, ...), condition=%wide.region_13.14_spmd, body=%wide.region_10.13_spmd.sunk | while | flops 402785056 | bytes 2625843 | solution.py:80
  301.9 2.2 fusion.80
  311.0 2.2 fusion.80
  320.1 2.2 fusion.80
  329.2 2.2 fusion.80
  338.3 2.2 fusion.80
  347.4 2.2 fusion.80
  356.5 2.2 fusion.80
  365.6 2.2 fusion.80
  (159 shorter events, 100.5 us)
Async XLA Ops:
  8.0 89.1 %copy-start = (f32[64,256]{1,0:T(8,128)S(1)}, f32[64,256]{1,0:T(8,128)}, u32[]{:S(2)}) copy-start(f32[64,256]{1,0:T(8,128)} %param.28) | copy-start | bytes 196612
  8.0 104.7 %reduce-scatter.2.cloned.1.call-start = ((), (), s32[]{:S(2)}) async-start(), calls=%async_computation.1 | async-start | bytes 327680 | tf_op jit(solution)/shard_map/reduce_scatter | solution.py:91
  8.1 1.7 copy-start.5
  8.1 1.7 copy-start.6
  8.1 1.7 copy-start.7
  9.8 80.1 %copy-start.3 = (f32[64,256]{1,0:T(8,128)S(1)}, f32[64,256]{1,0:T(8,128)}, u32[]{:S(2)}) copy-start(f32[64,256]{1,0:T(8,128)} %param.29) | copy-start | bytes 196612
  89.1 23.6 %copy-start.4 = (f32[64,256]{1,0:T(8,128)S(1)}, f32[64,256]{1,0:T(8,128)}, u32[]{:S(2)}) copy-start(f32[64,256]{1,0:T(8,128)} %param.27) | copy-start | bytes 196612
  89.8 64.6 %all-gather.9.cloned.1.call-start = ((), (), s32[]{:S(2)}) async-start(), calls=%async_computation.2 | async-start | bytes 2359296 | tf_op jit(solution)/shard_map/all_gather | solution.py:11
  103.7 100.7 %all-gather.11.cloned.1.call-start = ((), (), s32[]{:S(2)}) async-start(), calls=%async_computation.3 | async-start | bytes 2359296 | tf_op jit(solution)/shard_map/all_gather | solution.py:11
  125.9 138.4 %all-gather.13.cloned.1.call-start = ((), (), s32[]{:S(2)}) async-start(), calls=%async_computation.4 | async-start | bytes 2359296 | tf_op jit(solution)/shard_map/all_gather | solution.py:11
  204.4 1.0 copy-start.1
  204.4 1.0 copy-start.2
  207.1 84.4 %all-gather.15.cloned.1.call-start = ((), (), s32[]{:S(2)}) async-start(), calls=%async_computation.5 | async-start | bytes 1310720 | tf_op jit(solution)/shard_map/all_gather | solution.py:115
Sparse Core Ops, SparseCore 0:
  89.9 22.7 reduce-scatter.1
  277.5 13.9 all-gather.14
Sparse Core Ops, SparseCore 1:
  103.7 50.6 all-gather.8
  156.6 47.7 all-gather.10
  207.2 57.1 all-gather.12
